TPU v7x, 256 devices: a whole 4x4x8 slice. The times are simulated.
256 devices in a mesh: tm: 8 (over z_hi, y), space: 32 (over z_lo, x, core).
Axes of the slice: x: 4, y: 4, z: 8 (z_hi: 2, z_lo: 4; z = z_hi * 4 + z_lo), core: 2. Of those that a mesh axis runs over, the one named last changes fastest.
Arguments:
- member_average: float32 [128, 2880, 640], P('tm', 'space'), may hold values from -6 to 6
- member_spread_squared: float32 [128, 2880, 640], P('tm', 'space'), may hold values from 0.1 to 4
- measured_truth: float32 [128, 2880, 640], P('tm', 'space'), may hold values from -8 to 8
- coefficients: float32 [4, 2880, 640], P(None, 'space'), may hold values from -1 to 1
Outputs:
- updated: float32 [4, 2880, 640], P(None, 'space')
All inputs are finite; a program needn't handle non-finite values.
Results may differ from a plain program's by a relative error of at most 0.00002.
Values sent between devices are 32-bit elements; how exact they have to be, the bound alone decides.
No kernel may reach another device: no remote copies, remote signals or barrier semaphores. Data moves between devices by JAX's collectives and lax.ppermute only.
A program may use at most 64 MiB of HBM per device.

v0:
```python
import jax
import jax.numpy as jnp
from jax import lax
from jax.sharding import PartitionSpec as P

ITERS = 2
descent_factor = 0.5
smooth_weight = 0.03


def padded(block, sides, width):
    for axis, dim in sides:
        count = lax.axis_size(axis)
        forward = [(i, i + 1) for i in range(count - 1)]
        forward.append((count - 1, 0))
        backward = [(target, source) for source, target in forward]
        low = lax.ppermute(
            lax.slice_in_dim(block, block.shape[dim] - width, None, axis=dim), axis, forward
        )
        high = lax.ppermute(lax.slice_in_dim(block, 0, width, axis=dim), axis, backward)
        block = jnp.concatenate([low, block, high], axis=dim)
    return block


def laplace_rim(extended):
    middle = extended[:, 1:-1, :]
    along_lon = extended[:, 2:, :] + extended[:, :-2, :] - 2.0 * middle
    steps_lat = middle[..., 1:] - middle[..., :-1]
    zero_col = jnp.zeros(middle.shape[:-1] + (1,), jnp.float32)
    along_lat = jnp.concatenate([steps_lat, zero_col], axis=-1) - jnp.concatenate(
        [zero_col, steps_lat], axis=-1
    )
    return along_lon + along_lat


def daily_score_parts(calibration_coefficients_set, fmean, fvar, obs):
    base_exp = jnp.exp(calibration_coefficients_set[2])
    spread = jnp.sqrt(
        base_exp + calibration_coefficients_set[3] * calibration_coefficients_set[3] * fvar
    )
    center = calibration_coefficients_set[0] + calibration_coefficients_set[1] * fmean
    standard = (obs - center) / spread
    cumulative = 0.5 * (1.0 + jax.scipy.special.erf(standard * 0.7071067811865476))
    density = jnp.exp(-0.5 * standard * standard) * 0.3989422804014327
    dcenter = 1.0 - 2.0 * cumulative
    dvar = (2.0 * density - 0.5641895835477563) / (2.0 * spread)
    return jnp.stack(
        [
            jnp.sum(dcenter, axis=0),
            jnp.sum(dcenter * fmean, axis=0),
            jnp.sum(dvar * base_exp, axis=0),
            jnp.sum(dvar * 2.0 * calibration_coefficients_set[3] * fvar, axis=0),
        ]
    )


def smoothing(calibration_coefficients_set):
    first = laplace_rim(padded(calibration_coefficients_set, (("space", 1),), 1))
    return laplace_rim(padded(first, (("space", 1),), 1))


def apply_update(calibration_coefficients_set, partial_sum, roughness_cost, every_day_total):
    aggregate_loss = lax.psum(partial_sum, "tm")
    return calibration_coefficients_set - descent_factor * (
        aggregate_loss / every_day_total + roughness_cost
    )


def on_device(member_average, member_spread_squared, measured_truth, coefficients):
    calibration_coefficients_set = coefficients
    every_day_total = member_average.shape[0] * lax.axis_size("tm")
    for step in range(ITERS):
        partial_sum = daily_score_parts(
            calibration_coefficients_set, member_average, member_spread_squared, measured_truth
        )
        roughness_cost = smooth_weight * smoothing(calibration_coefficients_set)
        calibration_coefficients_set = apply_update(
            calibration_coefficients_set, partial_sum, roughness_cost, every_day_total
        )
    return calibration_coefficients_set


def solution(mesh):
    placed = (
        P("tm", "space", None),
        P("tm", "space", None),
        P("tm", "space", None),
        P(None, "space", None),
    )
    return jax.shard_map(
        on_device, mesh=mesh, in_specs=placed, out_specs=P(None, "space", None), check_vma=False
    )
```

profile of v0, /device:TPU:2, one launch (start us, length us, event | category | flops | bytes accessed | tf_op | source)
XLA Modules:
  0.0 270.6 jit_solution(1380413186751168871)
XLA Ops:
  6.5 0.0 all-reduce.11.cloned.1.call-start
  6.5 0.0 copy-start
  6.5 1.4 copy.16
  7.9 0.1 multiply_bitcast_fusion.2
  8.0 0.8 copy-done
  8.9 5.4 %add_subtract_fusion.1 = (f32[16,90,640]{2,0,1:T(8,128)S(1)}, f32[16,90,640]{2,0,1:T(8,128)S(1)}) fusion(f32[16,90,640]{2,0,1:T(8,128)} %param.5, f32[90,640]{1,0:T(8,128)S(1)} %get-tuple-element.27, f32[90,640]{1,0:T(8,128)S(1)} %get-tuple-element.28, f32[16,90,640]{2,0,1:T(8,128)} %param.6, f32[16,90,640]{2,0,1:T(8,128)S(1)} %copy-done, ...), kind=kLoop, calls=%fused_computation.19 | loop fusion | flops 8294400 | bytes 19353600 | tf_op jit(solution)/shard_map/sub | solution.py:45
  14.3 0.0 copy-start.2
  14.3 1.7 fusion.31
  15.9 0.4 copy-done.2
  16.3 4.6 %multiply_reduce_fusion.4 = (f32[90,640]{1,0:T(8,128)S(1)}, f32[90,640]{1,0:T(8,128)S(1)}) fusion(f32[90,640]{1,0:T(8,128)S(1)} %get-tuple-element.28, f32[16,90,640]{2,0,1:T(8,128)S(1)} %copy-done.2, f32[90,640]{1,0:T(8,128)S(1)} %get-tuple-element.27, f32[16,90,640]{2,0,1:T(8,128)S(1)} %get-tuple-element.16, f32[90,640]{1,0:T(8,128)S(1)} %get-tuple-element.26), kind=kLoop, calls=%fused_computation.17 | loop fusion | flops 11865600 | bytes 8524800 | tf_op jit(solution)/shard_map/reduce_sum | solution.py:51
  20.9 1.0 pad_maximum_fusion.8
  22.0 0.0 all-reduce.11.cloned.1.call-update
  22.0 0.0 all-reduce.13.cloned.1.call-start
  22.0 0.7 fusion.35
  22.8 0.1 collective-permute-start
  22.9 0.6 collective-permute-start.1
  23.5 0.3 slice_subtract_fusion.3
  23.8 0.5 collective-permute-done
  24.2 2.4 collective-permute-done.1
  26.7 0.4 fusion.27
  27.1 3.9 %collective-permute-start.2 = (f32[4,1,640]{2,1,0:T(1,128)S(1)}, f32[4,1,640]{2,1,0:T(1,128)S(1)}, u32[]{:S(2)}, u32[]{:S(2)}) collective-permute-start(f32[4,1,640]{2,1,0:T(1,128)S(1)} %get-tuple-element.31), channel_id=1, source_target_pairs={{1,0},{2,1},{3,2},{4,3},{5,4},{6,5},{7,6},{8,7},{9,8},{10,9},{11,1... | collective-permute-start | bytes 30728 | tf_op jit(solution)/shard_map/ppermute | solution.py:20
  31.1 0.0 collective-permute-start.3
  31.1 0.3 slice_subtract_fusion.2
  31.4 1.1 collective-permute-done.2
  32.4 6.3 %collective-permute-done.3 = f32[4,1,640]{2,1,0:T(1,128)S(1)} collective-permute-done((f32[4,1,640]{2,1,0:T(1,128)S(1)}, f32[4,1,640]{2,1,0:T(1,128)S(1)}, u32[]{:S(2)}, u32[]{:S(2)}) %collective-permute-start.3) | collective-permute-done | bytes 10272 | tf_op jit(solution)/shard_map/ppermute | solution.py:17
  38.7 98.3 %all-reduce.11.cloned.1.call-done = f32[4,90,640]{2,1,0:T(8,128)} async-done(((f32[4,90,640]{2,1,0:T(8,128)}), f32[4,90,640]{2,1,0:T(8,128)}) %all-reduce.11.cloned.1.call-update) | async-done | bytes 921616 | tf_op jit(solution)/shard_map/psum | solution.py:63
  137.1 0.0 copy-start.1
  137.1 2.2 fusion.24
  139.3 0.1 multiply_bitcast_fusion
  139.4 0.3 copy-done.1
  139.7 5.4 %add_subtract_fusion = (f32[16,90,640]{2,0,1:T(8,128)S(1)}, f32[16,90,640]{2,0,1:T(8,128)S(1)}) fusion(f32[16,90,640]{2,0,1:T(8,128)} %param.5, f32[90,640]{1,0:T(8,128)S(1)} %get-tuple-element.18, f32[90,640]{1,0:T(8,128)S(1)} %get-tuple-element.19, f32[16,90,640]{2,0,1:T(8,128)} %param.6, f32[16,90,640]{2,0,1:T(8,128)S(1)} %copy-done.1, ...), kind=kLoop, calls=%fused_computation.13 | loop fusion | flops 8294400 | bytes 19353600 | tf_op jit(solution)/shard_map/sub | solution.py:45
  145.1 0.0 copy-start.3
  145.1 1.7 fusion.30
  146.8 0.4 copy-done.3
  147.2 4.6 %multiply_reduce_fusion.1 = (f32[90,640]{1,0:T(8,128)S(1)}, f32[90,640]{1,0:T(8,128)S(1)}) fusion(f32[90,640]{1,0:T(8,128)S(1)} %get-tuple-element.19, f32[16,90,640]{2,0,1:T(8,128)S(1)} %copy-done.3, f32[90,640]{1,0:T(8,128)S(1)} %get-tuple-element.18, f32[16,90,640]{2,0,1:T(8,128)S(1)} %get-tuple-element.14, f32[90,640]{1,0:T(8,128)S(1)} %get-tuple-element.17), kind=kLoop, calls=%fused_computation.11 | loop fusion | flops 11865600 | bytes 8524800 | tf_op jit(solution)/shard_map/reduce_sum | solution.py:51
  151.8 1.0 pad_maximum_fusion.9
  152.8 0.0 all-reduce.13.cloned.1.call-update
  152.8 0.1 collective-permute-start.4
  152.9 0.5 collective-permute-start.5
  153.4 0.3 slice_subtract_fusion.1
  153.8 0.6 collective-permute-done.4
  154.3 1.8 collective-permute-done.5
  156.1 0.4 fusion.17
  156.6 0.1 collective-permute-start.6
  156.6 0.5 collective-permute-start.7
  157.1 0.3 slice_subtract_fusion
  157.5 0.6 collective-permute-done.6
  158.0 4.5 %collective-permute-done.7 = f32[4,1,640]{2,1,0:T(1,128)S(1)} collective-permute-done((f32[4,1,640]{2,1,0:T(1,128)S(1)}, f32[4,1,640]{2,1,0:T(1,128)S(1)}, u32[]{:S(2)}, u32[]{:S(2)}) %collective-permute-start.7) | collective-permute-done | bytes 10272 | tf_op jit(solution)/shard_map/ppermute | solution.py:17
  162.6 97.9 %all-reduce.13.cloned.1.call-done = f32[4,90,640]{2,1,0:T(8,128)} async-done(((f32[4,90,640]{2,1,0:T(8,128)}), f32[4,90,640]{2,1,0:T(8,128)}) %all-reduce.13.cloned.1.call-update) | async-done | bytes 921616 | tf_op jit(solution)/shard_map/psum | solution.py:63
  260.4 1.8 fusion.14
  262.2 1.5 copy.17
  (5 shorter events, 0.1 us)
Async XLA Ops:
  6.5 130.6 %all-reduce.11.cloned.1.call-start = ((), (), s32[]{:S(2)}) async-start(), calls=%async_computation | async-start | bytes 1966080 | tf_op jit(solution)/shard_map/psum | solution.py:63
  6.5 2.3 copy-start
  14.3 2.0 copy-start.2
  22.0 238.5 %all-reduce.13.cloned.1.call-start = ((), (), s32[]{:S(2)}) async-start(), calls=%async_computation.1 | async-start | bytes 1966080 | tf_op jit(solution)/shard_map/psum | solution.py:63
  22.8 1.5 collective-permute-start
  22.9 3.8 %collective-permute-start.1 = (f32[4,1,640]{2,1,0:T(1,128)S(1)}, f32[4,1,640]{2,1,0:T(1,128)S(1)}, u32[]{:S(2)}, u32[]{:S(2)}) collective-permute-start(f32[4,1,640]{2,1,0:T(1,128)S(1)} %copy.11), channel_id=1, source_target_pairs={{0,1},{1,2},{2,3},{3,4},{4,5},{5,6},{6,7},{7,8},{8,9},{9,10},{10,1... | collective-permute-start | bytes 30728 | tf_op jit(solution)/shard_map/ppermute | solution.py:17
  27.1 5.3 %collective-permute-start.2 = (f32[4,1,640]{2,1,0:T(1,128)S(1)}, f32[4,1,640]{2,1,0:T(1,128)S(1)}, u32[]{:S(2)}, u32[]{:S(2)}) collective-permute-start(f32[4,1,640]{2,1,0:T(1,128)S(1)} %get-tuple-element.31), channel_id=1, source_target_pairs={{1,0},{2,1},{3,2},{4,3},{5,4},{6,5},{7,6},{8,7},{9,8},{10,9},{11,1... | collective-permute-start | bytes 30728 | tf_op jit(solution)/shard_map/ppermute | solution.py:20
  31.1 7.7 %collective-permute-start.3 = (f32[4,1,640]{2,1,0:T(1,128)S(1)}, f32[4,1,640]{2,1,0:T(1,128)S(1)}, u32[]{:S(2)}, u32[]{:S(2)}) collective-permute-start(f32[4,1,640]{2,1,0:T(1,128)S(1)} %get-tuple-element.32), channel_id=1, source_target_pairs={{0,1},{1,2},{2,3},{3,4},{4,5},{5,6},{6,7},{7,8},{8,9},{9,10},{10,1... | collective-permute-start | bytes 30728 | tf_op jit(solution)/shard_map/ppermute | solution.py:17
  137.1 2.6 copy-start.1
  145.1 2.0 copy-start.3
  152.8 1.5 collective-permute-start.4
  152.9 3.2 %collective-permute-start.5 = (f32[4,1,640]{2,1,0:T(1,128)S(1)}, f32[4,1,640]{2,1,0:T(1,128)S(1)}, u32[]{:S(2)}, u32[]{:S(2)}) collective-permute-start(f32[4,1,640]{2,1,0:T(1,128)S(1)} %get-tuple-element.25), channel_id=1, source_target_pairs={{0,1},{1,2},{2,3},{3,4},{4,5},{5,6},{6,7},{7,8},{8,9},{9,10},{10,1... | collective-permute-start | bytes 30728 | tf_op jit(solution)/shard_map/ppermute | solution.py:17
  156.6 1.5 collective-permute-start.6
  156.6 5.9 %collective-permute-start.7 = (f32[4,1,640]{2,1,0:T(1,128)S(1)}, f32[4,1,640]{2,1,0:T(1,128)S(1)}, u32[]{:S(2)}, u32[]{:S(2)}) collective-permute-start(f32[4,1,640]{2,1,0:T(1,128)S(1)} %get-tuple-element.23), channel_id=1, source_target_pairs={{0,1},{1,2},{2,3},{3,4},{4,5},{5,6},{6,7},{7,8},{8,9},{9,10},{10,1... | collective-permute-start | bytes 30728 | tf_op jit(solution)/shard_map/ppermute | solution.py:17
Sparse Core Ops, SparseCore 0:
  22.1 114.9 all-reduce.10
  153.0 107.4 all-reduce.12
where the time goes:
time: 271 us
  waiting for transfers between devices  214 us (79%)
  other arithmetic  31.7 us (12%)
  between operations  13.6 us (5%)
  starting transfers between devices  5.8 us (2%)
  local copies, waits for them, and re-layouts  5.58 us (2%)
    psum x2, waiting for transfers between devices, apply_update(): aggregate_loss = lax.psum(partial_sum, 'tm')  196 us
    ppermute x4, waiting for transfers between devices, padded(): lax.ppermute(lax.slice_in_dim(block, block.shape[dim] - width, None, axis...  15.1 us
    sub x2, other arithmetic, daily_score_parts(): dcenter = 1.0 - 2.0 * cumulative  10.8 us
    reduce_sum x2, other arithmetic, daily_score_parts(): jnp.sum(dvar * base_exp, axis=0)  9.22 us
  transfers between devices with their start and end apart: 10, of which 10 were waited for; matrix products, arithmetic and copies ran while one was open for 1% of the time, Pallas kernels for 0%

commit v1 on v0

--- a/solution.py
+++ b/solution.py
@@ -60,7 +60,7 @@
 
 
 def apply_update(calibration_coefficients_set, partial_sum, roughness_cost, every_day_total):
-    aggregate_loss = lax.psum(partial_sum, "tm")
+    aggregate_loss = jnp.sum(lax.all_gather(partial_sum, "tm"), axis=0)
     return calibration_coefficients_set - descent_factor * (
         aggregate_loss / every_day_total + roughness_cost
     )

time: 271 us -> 385 us (1.42)
  waiting for transfers between devices: 214 us -> 318 us
  other arithmetic: 31.7 us -> 41.4 us
    all_gather x0 -> x2, waiting for transfers between devices: none -> 313 us  [apply_update(): aggregate_loss = jnp.sum(lax.all_gather(partial_sum, 'tm'), axis=0)]
    psum x2 -> x0, waiting for transfers between devices: 196 us -> none  [apply_update(): aggregate_loss = lax.psum(partial_sum, 'tm')]
    ppermute x4, waiting for transfers between devices: 15.1 us -> 4.22 us  [padded(): lax.ppermute(lax.slice_in_dim(block, block.shape[dim] - width, None, axis...]
    reduce_sum x0 -> x2, other arithmetic: none -> 9.58 us  [apply_update(): aggregate_loss = jnp.sum(lax.all_gather(partial_sum, 'tm'), axis=0)]
  transfers between devices with their start and end apart: 10 -> 10, of which waited for: 10 -> 6; matrix products, arithmetic and copies ran while one was open for 1% -> 3% of each run, Pallas kernels for 0% -> 0%
where the time goes in v1:
time: 385 us
  waiting for transfers between devices  318 us (83%)
  other arithmetic  41.4 us (11%)
  between operations  13.6 us (4%)
  starting transfers between devices  5.8 us (2%)
  local copies, waits for them, and re-layouts  5.6 us (1%)
    all_gather x2, waiting for transfers between devices, apply_update(): aggregate_loss = jnp.sum(lax.all_gather(partial_sum, 'tm'), axis=0)  313 us
    sub x2, other arithmetic, daily_score_parts(): dcenter = 1.0 - 2.0 * cumulative  10.8 us
    reduce_sum x2, other arithmetic, apply_update(): aggregate_loss = jnp.sum(lax.all_gather(partial_sum, 'tm'), axis=0)  9.58 us
    reduce_sum x2, other arithmetic, daily_score_parts(): jnp.sum(dvar * base_exp, axis=0)  9.22 us
  transfers between devices with their start and end apart: 10, of which 6 were waited for; matrix products, arithmetic and copies ran while one was open for 3% of the time, Pallas kernels for 0%

profile of v1, /device:TPU:2, one launch (start us, length us, event | category | flops | bytes accessed | tf_op | source)
XLA Modules:
  0.0 384.8 jit_solution(7305542938247314441)
XLA Ops:
  6.5 0.0 all-gather.5.cloned.1.call-start
  6.5 0.0 copy-start
  6.5 1.4 copy.29
  7.9 0.1 multiply_bitcast_fusion.2
  8.0 0.8 copy-done
  8.9 5.4 %add_subtract_fusion.1 = (f32[16,90,640]{2,0,1:T(8,128)S(1)}, f32[16,90,640]{2,0,1:T(8,128)S(1)}) fusion(f32[16,90,640]{2,0,1:T(8,128)} %param.5, f32[90,640]{1,0:T(8,128)S(1)} %get-tuple-element.27, f32[90,640]{1,0:T(8,128)S(1)} %get-tuple-element.28, f32[16,90,640]{2,0,1:T(8,128)} %param.6, f32[16,90,640]{2,0,1:T(8,128)S(1)} %copy-done, ...), kind=kLoop, calls=%fused_computation.19 | loop fusion | flops 8294400 | bytes 19353600 | tf_op jit(solution)/shard_map/sub | solution.py:45
  14.3 0.0 copy-start.2
  14.3 1.7 fusion.31
  15.9 0.4 copy-done.2
  16.3 4.6 %multiply_reduce_fusion.4 = (f32[90,640]{1,0:T(8,128)S(1)}, f32[90,640]{1,0:T(8,128)S(1)}) fusion(f32[90,640]{1,0:T(8,128)S(1)} %get-tuple-element.28, f32[16,90,640]{2,0,1:T(8,128)S(1)} %copy-done.2, f32[90,640]{1,0:T(8,128)S(1)} %get-tuple-element.27, f32[16,90,640]{2,0,1:T(8,128)S(1)} %get-tuple-element.16, f32[90,640]{1,0:T(8,128)S(1)} %get-tuple-element.26), kind=kLoop, calls=%fused_computation.17 | loop fusion | flops 11865600 | bytes 8524800 | tf_op jit(solution)/shard_map/reduce_sum | solution.py:51
  20.9 1.1 pad_maximum_fusion.8
  22.1 0.0 all-gather.5.cloned.1.call-update
  22.1 0.0 all-gather.7.cloned.1.call-start
  22.1 0.7 fusion.35
  22.9 0.1 collective-permute-start
  23.0 0.6 collective-permute-start.1
  23.5 0.3 slice_subtract_fusion.3
  23.9 0.5 collective-permute-done
  24.3 2.4 collective-permute-done.1
  26.8 0.4 fusion.27
  27.2 3.9 %collective-permute-start.2 = (f32[4,1,640]{2,1,0:T(1,128)S(1)}, f32[4,1,640]{2,1,0:T(1,128)S(1)}, u32[]{:S(2)}, u32[]{:S(2)}) collective-permute-start(f32[4,1,640]{2,1,0:T(1,128)S(1)} %get-tuple-element.31), channel_id=1, source_target_pairs={{1,0},{2,1},{3,2},{4,3},{5,4},{6,5},{7,6},{8,7},{9,8},{10,9},{11,1... | collective-permute-start | bytes 30728 | tf_op jit(solution)/shard_map/ppermute | solution.py:20
  31.1 0.0 collective-permute-start.3
  31.2 0.3 slice_subtract_fusion.2
  31.5 158.4 %all-gather.5.cloned.1.call-done = f32[32,90,640]{2,1,0:T(8,128)} async-done(((f32[4,90,640]{2,1,0:T(8,128)}), f32[32,90,640]{2,1,0:T(8,128)}) %all-gather.5.cloned.1.call-update) | async-done | bytes 7372816 | tf_op jit(solution)/shard_map/all_gather | solution.py:63
  189.8 4.8 %reduce_sum.94 = f32[4,90,640]{2,1,0:T(8,128)} reduce(f32[8,4,90,640]{3,2,1,0:T(8,128)} %bitcast.30, f32[]{:T(128)} %constant.12.clone.1), dimensions={0}, to_apply=%region_4.0 | reduce | flops 1612800 | bytes 8294404 | tf_op jit(solution)/shard_map/reduce_sum | solution.py:63
  194.6 0.0 copy-start.1
  194.6 0.0 collective-permute-done.2
  194.6 0.0 collective-permute-done.3
  194.6 2.2 fusion.24
  196.8 0.1 multiply_bitcast_fusion
  196.9 0.3 copy-done.1
  197.2 5.4 %add_subtract_fusion = (f32[16,90,640]{2,0,1:T(8,128)S(1)}, f32[16,90,640]{2,0,1:T(8,128)S(1)}) fusion(f32[16,90,640]{2,0,1:T(8,128)} %param.5, f32[90,640]{1,0:T(8,128)S(1)} %get-tuple-element.18, f32[90,640]{1,0:T(8,128)S(1)} %get-tuple-element.19, f32[16,90,640]{2,0,1:T(8,128)} %param.6, f32[16,90,640]{2,0,1:T(8,128)S(1)} %copy-done.1, ...), kind=kLoop, calls=%fused_computation.13 | loop fusion | flops 8294400 | bytes 19353600 | tf_op jit(solution)/shard_map/sub | solution.py:45
  202.6 0.0 copy-start.3
  202.6 1.7 fusion.30
  204.3 0.4 copy-done.3
  204.7 4.6 %multiply_reduce_fusion.1 = (f32[90,640]{1,0:T(8,128)S(1)}, f32[90,640]{1,0:T(8,128)S(1)}) fusion(f32[90,640]{1,0:T(8,128)S(1)} %get-tuple-element.19, f32[16,90,640]{2,0,1:T(8,128)S(1)} %copy-done.3, f32[90,640]{1,0:T(8,128)S(1)} %get-tuple-element.18, f32[16,90,640]{2,0,1:T(8,128)S(1)} %get-tuple-element.14, f32[90,640]{1,0:T(8,128)S(1)} %get-tuple-element.17), kind=kLoop, calls=%fused_computation.11 | loop fusion | flops 11865600 | bytes 8524800 | tf_op jit(solution)/shard_map/reduce_sum | solution.py:51
  209.3 1.1 pad_maximum_fusion.9
  210.4 0.0 all-gather.7.cloned.1.call-update
  210.5 0.1 collective-permute-start.4
  210.6 0.5 collective-permute-start.5
  211.1 0.3 slice_subtract_fusion.1
  211.4 0.6 collective-permute-done.4
  212.0 1.8 collective-permute-done.5
  213.8 0.4 fusion.17
  214.2 0.1 collective-permute-start.6
  214.3 0.5 collective-permute-start.7
  214.8 0.3 slice_subtract_fusion
  215.1 154.7 %all-gather.7.cloned.1.call-done = f32[32,90,640]{2,1,0:T(8,128)} async-done(((f32[4,90,640]{2,1,0:T(8,128)}), f32[32,90,640]{2,1,0:T(8,128)}) %all-gather.7.cloned.1.call-update) | async-done | bytes 7372816 | tf_op jit(solution)/shard_map/all_gather | solution.py:63
  369.8 4.8 %reduce_sum.99 = f32[4,90,640]{2,1,0:T(8,128)} reduce(f32[8,4,90,640]{3,2,1,0:T(8,128)} %bitcast.31, f32[]{:T(128)} %constant.12.clone.1), dimensions={0}, to_apply=%region_9.0 | reduce | flops 1612800 | bytes 8294404 | tf_op jit(solution)/shard_map/reduce_sum | solution.py:63
  374.6 0.0 collective-permute-done.6
  374.6 0.0 collective-permute-done.7
  374.6 1.8 fusion.14
  376.4 1.5 copy.30
  (5 shorter events, 0.1 us)
Async XLA Ops:
  6.5 183.3 %all-gather.5.cloned.1.call-start = ((), (), s32[]{:S(2)}) async-start(), calls=%async_computation | async-start | bytes 8847360 | tf_op jit(solution)/shard_map/all_gather | solution.py:63
  6.5 2.3 copy-start
  14.3 2.0 copy-start.2
  22.1 347.8 %all-gather.7.cloned.1.call-start = ((), (), s32[]{:S(2)}) async-start(), calls=%async_computation.1 | async-start | bytes 8847360 | tf_op jit(solution)/shard_map/all_gather | solution.py:63
  22.9 1.5 collective-permute-start
  23.0 3.8 collective-permute-start.1
  27.2 167.4 %collective-permute-start.2 = (f32[4,1,640]{2,1,0:T(1,128)S(1)}, f32[4,1,640]{2,1,0:T(1,128)S(1)}, u32[]{:S(2)}, u32[]{:S(2)}) collective-permute-start(f32[4,1,640]{2,1,0:T(1,128)S(1)} %get-tuple-element.31), channel_id=1, source_target_pairs={{1,0},{2,1},{3,2},{4,3},{5,4},{6,5},{7,6},{8,7},{9,8},{10,9},{11,1... | collective-permute-start | bytes 30728 | tf_op jit(solution)/shard_map/ppermute | solution.py:20
  31.1 163.5 %collective-permute-start.3 = (f32[4,1,640]{2,1,0:T(1,128)S(1)}, f32[4,1,640]{2,1,0:T(1,128)S(1)}, u32[]{:S(2)}, u32[]{:S(2)}) collective-permute-start(f32[4,1,640]{2,1,0:T(1,128)S(1)} %get-tuple-element.32), channel_id=1, source_target_pairs={{0,1},{1,2},{2,3},{3,4},{4,5},{5,6},{6,7},{7,8},{8,9},{9,10},{10,1... | collective-permute-start | bytes 30728 | tf_op jit(solution)/shard_map/ppermute | solution.py:17
  194.6 2.6 copy-start.1
  202.6 2.0 copy-start.3
  210.5 1.5 collective-permute-start.4
  210.6 3.2 collective-permute-start.5
  214.2 160.4 %collective-permute-start.6 = (f32[4,1,640]{2,1,0:T(1,128)S(1)}, f32[4,1,640]{2,1,0:T(1,128)S(1)}, u32[]{:S(2)}, u32[]{:S(2)}) collective-permute-start(f32[4,1,640]{2,1,0:T(1,128)S(1)} %get-tuple-element.22), channel_id=1, source_target_pairs={{1,0},{2,1},{3,2},{4,3},{5,4},{6,5},{7,6},{8,7},{9,8},{10,9},{11,1... | collective-permute-start | bytes 30728 | tf_op jit(solution)/shard_map/ppermute | solution.py:20
  214.3 160.3 %collective-permute-start.7 = (f32[4,1,640]{2,1,0:T(1,128)S(1)}, f32[4,1,640]{2,1,0:T(1,128)S(1)}, u32[]{:S(2)}, u32[]{:S(2)}) collective-permute-start(f32[4,1,640]{2,1,0:T(1,128)S(1)} %get-tuple-element.23), channel_id=1, source_target_pairs={{0,1},{1,2},{2,3},{3,4},{4,5},{5,6},{6,7},{7,8},{8,9},{9,10},{10,1... | collective-permute-start | bytes 30728 | tf_op jit(solution)/shard_map/ppermute | solution.py:17
Sparse Core Ops, SparseCore 0:
  22.2 167.5 all-gather.4
  210.6 159.2 all-gather.6
